TPU v7x, 32 devices: a whole 2x2x4 slice. The times are simulated.
32 devices in a mesh: dp: 16 (over z, x, core), mp: 2 (over y).
Axes of the slice: x: 2, y: 2, z: 4, core: 2. Of those that a mesh axis runs over, the one named last changes fastest.
Arguments:
- features: bfloat16 [2048, 512], P('dp'), may hold values from -6 to 6
- w_in: bfloat16 [512, 512], P(None, 'mp'), may hold values from -0.25 to 0.25
- b_in: float32 [512], P('mp'), may hold values from -1 to 1
- w_out: bfloat16 [512, 128], P('mp'), may hold values from -0.25 to 0.25
- partner: int32 [2048], P('dp'), may hold values from 0 to 2047, as said below
- window: int32 [16], replicated, may hold values from 0 to 3
Outputs:
- row_loss: float32 [512], P('dp')
- grad_w_in: float32 [512, 512], P(None, 'mp')
- grad_b_in: float32 [512], P('mp')
- grad_w_out: float32 [512, 128], P('mp')
Inputs may be any that keep to these rules, and one draw needn't show every extreme that they name: partner pairs the rows: partner[partner[i]] = i and partner[i] != i for every row i.
All inputs are finite; a program needn't handle non-finite values.
Results may differ from a plain program's by a relative error of at most 0.0027.
Values may be sent and summed in bfloat16 or wider, within the bound.
A program may use at most 64 MiB of HBM per device.

v0:
```python
import math
import jax
import jax.numpy as jnp
from jax import lax
from jax.sharding import PartitionSpec as P

A_DEV = 32
INV_TEMP = 10.0
SHIFT = 10.0
EPS = 1e-06


def contract_rows(left, right):
    return lax.dot_general(
        left, right, (((0,), (0,)), ((), ())), preferred_element_type=jnp.float32
    )


def on_device(features, w_in, b_in, w_out, partner, window):
    rows = features.shape[0]
    parts = lax.axis_size("mp")
    part = lax.axis_index("mp")
    shards = lax.axis_size("dp")
    shard = lax.axis_index("dp")
    width = rows // parts
    anchor_rows = A_DEV
    anchor_all = anchor_rows * shards
    pre = jnp.dot(features, w_in, preferred_element_type=jnp.float32) + b_in
    hidden = jax.nn.silu(pre).astype(jnp.bfloat16)
    proj = lax.psum(jnp.dot(hidden, w_out, preferred_element_type=jnp.float32), "mp")
    norm = jnp.sqrt(jnp.sum(proj * proj, axis=1, keepdims=True) + EPS)
    emb = (proj / norm).astype(jnp.bfloat16)
    embed = emb.shape[1]
    own_cols = lax.dynamic_slice_in_dim(emb, part * width, width, 0)
    columns = lax.all_gather(own_cols, "dp", axis=0, tiled=True)
    col_total = columns.shape[0]
    shard_ids = jnp.arange(shards, dtype=jnp.int32)
    my_block = jnp.sum(jnp.where(shard_ids == shard, window, 0))
    my_start = my_block * anchor_rows
    anchors = lax.dynamic_slice_in_dim(emb, my_start, anchor_rows, 0)
    anchor_partner = lax.dynamic_slice_in_dim(partner, my_start, anchor_rows, 0)
    anchor_ids = shard * rows + my_start + jnp.arange(anchor_rows, dtype=jnp.int32)

    def column_ids(start, count):
        local = start + jnp.arange(count, dtype=jnp.int32)
        return local // width * rows + part * width + local % width

    blk = math.gcd(col_total, 2048)
    nblk = col_total // blk
    col_blocks = columns.reshape(nblk, blk, embed)
    starts = jnp.arange(nblk, dtype=jnp.int32) * blk

    def forward(carry, item):
        total, hit = carry
        block, start = item
        s = jnp.dot(anchors, block.T, preferred_element_type=jnp.float32) * INV_TEMP
        ids = column_ids(start, blk)
        ex = jnp.where(ids[None, :] == anchor_ids[:, None], 0.0, jnp.exp(s - SHIFT))
        hit = hit + jnp.sum(jnp.where(ids[None, :] == anchor_partner[:, None], s, 0.0), axis=1)
        return ((total + jnp.sum(ex, axis=1), hit), None)

    zero_rows = jnp.zeros((anchor_rows,), jnp.float32)
    (total, hit), _ = lax.scan(forward, (zero_rows, zero_rows), (col_blocks, starts))
    total, hit = lax.psum((total, hit), "mp")
    row_loss = jnp.log(total) + SHIFT - hit

    def row_weights(s, ids):
        prob = jnp.where(
            ids[None, :] == anchor_ids[:, None], 0.0, jnp.exp(s - SHIFT) / total[:, None]
        )
        onehot = (ids[None, :] == anchor_partner[:, None]).astype(jnp.float32)
        return (prob - onehot).astype(jnp.bfloat16)

    def backward(acc, item):
        block, start = item
        s = jnp.dot(anchors, block.T, preferred_element_type=jnp.float32) * INV_TEMP
        weights = row_weights(s, column_ids(start, blk))
        return (acc + jnp.dot(weights, block, preferred_element_type=jnp.float32), None)

    row_part, _ = lax.scan(
        backward, jnp.zeros((anchor_rows, embed), jnp.float32), (col_blocks, starts)
    )
    totals = lax.all_gather(total, "dp", axis=0, tiled=True)
    own_ids = shard * rows + part * width + jnp.arange(width, dtype=jnp.int32)
    own_partner = lax.dynamic_slice_in_dim(partner, part * width, width, 0)
    piece = lax.all_gather(anchors, "dp", axis=0, tiled=True)
    count = piece.shape[0]
    inner = math.gcd(count, 2048)
    sub_pieces = piece.reshape(count // inner, inner, embed)
    offsets = jnp.arange(count // inner, dtype=jnp.int32) * inner

    def one_block(inner_acc, item):
        block, offset = item
        block_totals = lax.dynamic_slice_in_dim(totals, offset, inner, 0)
        flat = offset + jnp.arange(inner, dtype=jnp.int32)
        owner = flat // anchor_rows
        owner_block = jnp.sum(
            jnp.where(owner[:, None] == shard_ids[None, :], window[None, :], 0), axis=1
        )
        ids = owner * rows + owner_block * anchor_rows + flat % anchor_rows
        s = jnp.dot(own_cols, block.T, preferred_element_type=jnp.float32) * INV_TEMP
        prob = jnp.where(
            ids[None, :] == own_ids[:, None], 0.0, jnp.exp(s - SHIFT) / block_totals[None, :]
        )
        onehot = (ids[None, :] == own_partner[:, None]).astype(jnp.float32)
        weights = (prob - onehot).astype(jnp.bfloat16)
        return (inner_acc + jnp.dot(weights, block, preferred_element_type=jnp.float32), None)

    result, _ = lax.scan(one_block, jnp.zeros((width, embed), jnp.float32), (sub_pieces, offsets))
    placed = lax.dynamic_update_slice_in_dim(
        jnp.zeros((rows, embed), jnp.float32), result, part * width, 0
    )
    row_placed = lax.dynamic_update_slice_in_dim(
        jnp.zeros((rows, embed), jnp.float32), row_part, my_start, 0
    )
    grad_emb = lax.psum(row_placed + placed, "mp") * (INV_TEMP / anchor_all)
    unit = proj / norm
    grad_proj = ((grad_emb - unit * jnp.sum(unit * grad_emb, axis=1, keepdims=True)) / norm).astype(
        jnp.bfloat16
    )
    grad_w_out = contract_rows(hidden, grad_proj)
    grad_hidden = lax.dot_general(
        grad_proj, w_out, (((1,), (1,)), ((), ())), preferred_element_type=jnp.float32
    )
    sig = jax.nn.sigmoid(pre)
    grad_pre = (grad_hidden * sig * (1.0 + pre * (1.0 - sig))).astype(jnp.bfloat16)
    grad_w_in = contract_rows(features, grad_pre)
    grad_b_in = jnp.sum(grad_pre.astype(jnp.float32), axis=0)
    grad_w_in, grad_b_in, grad_w_out = lax.psum((grad_w_in, grad_b_in, grad_w_out), "dp")
    return (row_loss, grad_w_in, grad_b_in, grad_w_out)


def solution(mesh):
    return jax.shard_map(
        on_device,
        mesh=mesh,
        in_specs=(P("dp", None), P(None, "mp"), P("mp"), P("mp", None), P("dp"), P()),
        out_specs=(P("dp"), P(None, "mp"), P("mp"), P("mp", None)),
        check_vma=False,
    )
```

profile of v0, /device:TPU:0, one launch (start us, length us, event | category | flops | bytes accessed | tf_op | source)
XLA Modules:
  0.0 234.8 jit_solution(11536599049466594532)
XLA Ops:
  7.2 0.0 copy-start
  7.2 0.0 copy-start.6
  7.2 0.0 all-reduce.7.cloned.1.call-start
  7.2 0.9 copy-done
  8.1 1.1 multiply_convert_fusion
  9.2 0.0 copy-done.6
  9.3 0.8 fusion.57
  10.0 0.0 all-reduce.7.cloned.1.call-update
  10.1 0.0 all-reduce.9.cloned.1.call-start
  10.1 0.0 copy-start.7
  10.1 0.6 copy-done.7
  10.8 0.6 fusion.50
  12.1 0.0 copy-start.8
  12.1 0.6 copy-done.8
  12.8 0.1 dynamic_slice.31
  12.8 0.1 dynamic_slice.32
  12.9 0.1 select_reduce_fusion
  13.0 0.0 copy-start.9
  13.0 0.6 copy-done.9
  13.7 0.6 dynamic-slice.3
  14.9 19.6 %all-reduce.7.cloned.1.call-done = f32[128,128]{1,0:T(8,128)} async-done(((f32[128,128]{1,0:T(8,128)}), f32[128,128]{1,0:T(8,128)}) %all-reduce.7.cloned.1.call-update) | async-done | bytes 65552 | tf_op jit(solution)/shard_map/psum | solution.py:30
  34.5 0.0 copy-start.1
  34.5 1.0 multiply_reduce_fusion.1
  35.6 0.0 copy-done.1
  35.6 0.1 fusion.56
  35.7 21.7 %all_gather.10 = bf16[512,128]{1,0:T(8,128)(2,1)S(1)} all-gather(bf16[32,128]{1,0:T(8,128)(2,1)S(1)} %constant_dynamic-slice_fusion.1), channel_id=1, replica_groups=mesh['dp'=16,'mp'=2] {'dp'}, dimensions={0}, use_global_device_ids=true | all-gather | bytes 139264 | tf_op jit(solution)/shard_map/all_gather | solution.py:86
  57.4 18.1 %all_gather.9 = bf16[1024,128]{1,0:T(8,128)(2,1)S(1)} all-gather(bf16[64,128]{1,0:T(8,128)(2,1)S(1)} %constant_dynamic-slice_fusion), channel_id=1, replica_groups=mesh['dp'=16,'mp'=2] {'dp'}, dimensions={0}, use_global_device_ids=true | all-gather | bytes 278528 | tf_op jit(solution)/shard_map/all_gather | solution.py:35
  75.5 0.3 fusion.11
  75.8 4.9 %all-reduce.2 = (f32[32]{0:T(128)S(1)}, f32[32]{0:T(128)S(1)}) all-reduce(f32[32]{0:T(128)S(1)} %get-tuple-element.70, f32[32]{0:T(128)S(1)} %get-tuple-element.69), channel_id=1, replica_groups=mesh['dp'=16,'mp'=2] {'mp'}, use_global_device_ids=true, to_apply=%region_6.7 | all-reduce | flops 64 | bytes 512 | tf_op jit(solution)/shard_map/psum | solution.py:64
  80.8 0.2 dynamic-update-slice.1
  81.0 29.9 %all-reduce = f32[512]{0:T(512)S(1)} all-reduce(f32[512]{0:T(512)S(1)} %dynamic-update-slice.1), channel_id=1, replica_groups=mesh['dp'=16,'mp'=2] {'dp'}, use_global_device_ids=true, to_apply=%add | all-reduce | flops 512 | bytes 4096
  110.9 0.2 convolution_dynamic-update-slice_fusion
  111.1 0.3 fusion.10
  111.4 0.0 copy-start.3
  111.5 0.6 copy-done.3
  112.1 0.0 all-reduce.9.cloned.1.call-update
  112.1 0.0 all-reduce.11.cloned.1.call-start
  112.2 17.4 %all-reduce.9.cloned.1.call-done = f32[128,128]{1,0:T(8,128)} async-done(((f32[128,128]{1,0:T(8,128)}), f32[128,128]{1,0:T(8,128)}) %all-reduce.9.cloned.1.call-update) | async-done | bytes 65552 | tf_op jit(solution)/shard_map/psum | solution.py:116
  129.6 0.0 copy-start.2
  129.6 1.1 multiply_reduce_fusion
  130.6 0.0 copy-done.2
  130.7 0.1 divide_convert_fusion
  130.8 0.9 fusion.58
  131.6 0.0 copy-start.5
  131.6 0.2 convert_reduce_fusion
  131.8 0.7 copy-done.5
  132.5 1.0 convolution_bitcast_fusion
  133.6 0.0 all-reduce.11.cloned.1.call-update
  133.6 0.5 add_subtract_fusion
  134.1 33.6 %psum.54 = f32[256]{0:T(256)} all-reduce(f32[256]{0:T(256)S(1)} %get-tuple-element.87), channel_id=1, replica_groups=mesh['dp'=16,'mp'=2] {'dp'}, use_global_device_ids=true, to_apply=%region_12.13 | all-reduce | flops 256 | bytes 2048 | tf_op jit(solution)/shard_map/psum | solution.py:129
  167.7 57.9 %all-reduce.11.cloned.1.call-done = (f32[512,256]{0,1:T(8,128)}, f32[256,128]{1,0:T(8,128)}) async-done(((f32[512,256]{0,1:T(8,128)}, f32[256,128]{1,0:T(8,128)}), (f32[512,256]{0,1:T(8,128)}, f32[256,128]{1,0:T(8,128)})) %all-reduce.11.cloned.1.call-update) | async-done | bytes 655376 | tf_op jit(solution)/shard_map/psum | solution.py:129
  225.5 0.0 copy-start.4
  225.5 2.1 copy.11
  227.6 0.0 copy-done.4
  227.6 0.7 copy.19
  (10 shorter events, 0.1 us)
Async XLA Ops:
  7.2 1.0 copy-start
  7.2 2.1 copy-start.6
  7.2 27.3 %all-reduce.7.cloned.1.call-start = ((), (), s32[]{:S(2)}) async-start(), calls=%async_computation | async-start | bytes 131072 | tf_op jit(solution)/shard_map/psum | solution.py:30
  10.1 119.5 %all-reduce.9.cloned.1.call-start = ((), (), s32[]{:S(2)}) async-start(), calls=%async_computation.1 | async-start | bytes 131072 | tf_op jit(solution)/shard_map/psum | solution.py:116
  10.1 0.7 copy-start.7
  12.1 0.7 copy-start.8
  13.0 0.7 copy-start.9
  34.5 1.0 copy-start.1
  111.4 0.6 copy-start.3
  112.1 113.4 %all-reduce.11.cloned.1.call-start = ((), (), s32[]{:S(2)}) async-start(), calls=%async_computation.2 | async-start | bytes 1310720 | tf_op jit(solution)/shard_map/psum | solution.py:129
  129.6 1.1 copy-start.2
  131.6 0.9 copy-start.5
  225.5 2.1 copy-start.4
Sparse Core Ops, SparseCore 0:
  10.8 23.6 all-reduce.6
  112.2 17.2 all-reduce.8
  133.7 91.7 all-reduce.10
where the time goes:
time: 235 us
  blocking collectives  108 us (46%)
  waiting for transfers between devices  94.9 us (40%)
  between operations  15.3 us (7%)
  local copies, waits for them, and re-layouts  7.86 us (3%)
  matrix products  4.84 us (2%)
  other arithmetic  3.56 us (2%)
    psum x1, waiting for transfers between devices, on_device(): lax.psum((grad_w_in, grad_b_in, grad_w_out), 'dp')  57.9 us
    psum x1, blocking collectives, on_device(): lax.psum((grad_w_in, grad_b_in, grad_w_out), 'dp')  33.6 us
    unnamed x1, blocking collectives  29.9 us
    all_gather x1, blocking collectives, on_device(): piece = lax.all_gather(anchors, 'dp', axis=0, tiled=True)  21.7 us
    psum x1, waiting for transfers between devices, on_device(): lax.psum(jnp.dot(hidden, w_out, preferred_element_type=jnp.float32), 'mp')  19.6 us
    all_gather x1, blocking collectives, on_device(): columns = lax.all_gather(own_cols, 'dp', axis=0, tiled=True)  18.1 us
    psum x1, waiting for transfers between devices, on_device(): grad_emb = lax.psum(row_placed + placed, 'mp') * (INV_TEMP / anchor_all)  17.4 us
    unnamed x25, local copies, waits for them, and re-layouts  7.68 us
  transfers between devices with their start and end apart: 3, of which 3 were waited for; matrix products, arithmetic and copies ran while one was open for 1% of the time, Pallas kernels for 0%

commit v1 on v0

--- a/solution.py
+++ b/solution.py
@@ -113,7 +113,7 @@
     row_placed = lax.dynamic_update_slice_in_dim(
         jnp.zeros((rows, embed), jnp.float32), row_part, my_start, 0
     )
-    grad_emb = lax.psum(row_placed + placed, "mp") * (INV_TEMP / anchor_all)
+    grad_emb = jnp.sum(lax.all_gather(row_placed + placed, "mp"), axis=0) * (INV_TEMP / anchor_all)
     unit = proj / norm
     grad_proj = ((grad_emb - unit * jnp.sum(unit * grad_emb, axis=1, keepdims=True)) / norm).astype(
         jnp.bfloat16

time: 235 us -> 218 us (0.928)
  waiting for transfers between devices: 94.9 us -> 77.2 us
    psum x1 -> x0, waiting for transfers between devices: 17.4 us -> none  [on_device(): grad_emb = lax.psum(row_placed + placed, 'mp') * (INV_TEMP / anchor_all)]
    all_gather x0 -> x1, blocking collectives: none -> 4.93 us  [on_device(): lax.all_gather(row_placed + placed, 'mp')]
    psum x1, blocking collectives: 33.6 us -> 30.2 us  [on_device(): lax.psum((grad_w_in, grad_b_in, grad_w_out), 'dp')]
    unnamed x25 -> x22, local copies, waits for them, and re-layouts: 7.68 us -> 7.06 us
  transfers between devices with their start and end apart: 3 -> 2, of which waited for: 3 -> 2; matrix products, arithmetic and copies ran while one was open for 1% -> 1% of each run, Pallas kernels for 0% -> 0%
where the time goes in v1:
time: 218 us; the launch traced here: 217 us
  blocking collectives  110 us (50%)
  waiting for transfers between devices  77.2 us (35%)
  between operations  15.5 us (7%)
  local copies, waits for them, and re-layouts  7.23 us (3%)
  matrix products  4.86 us (2%)
  other arithmetic  2.68 us (1%)
    psum x1, waiting for transfers between devices, on_device(): lax.psum((grad_w_in, grad_b_in, grad_w_out), 'dp')  57.6 us
    psum x1, blocking collectives, on_device(): lax.psum((grad_w_in, grad_b_in, grad_w_out), 'dp')  30.2 us
    unnamed x1, blocking collectives  29.9 us
    all_gather x1, blocking collectives, on_device(): piece = lax.all_gather(anchors, 'dp', axis=0, tiled=True)  21.7 us
    psum x1, waiting for transfers between devices, on_device(): lax.psum(jnp.dot(hidden, w_out, preferred_element_type=jnp.float32), 'mp')  19.6 us
    all_gather x1, blocking collectives, on_device(): columns = lax.all_gather(own_cols, 'dp', axis=0, tiled=True)  18.1 us
    unnamed x22, local copies, waits for them, and re-layouts  7.06 us
    all_gather x1, blocking collectives, on_device(): lax.all_gather(row_placed + placed, 'mp')  4.93 us
  transfers between devices with their start and end apart: 2, of which 2 were waited for; matrix products, arithmetic and copies ran while one was open for 1% of the time, Pallas kernels for 0%

profile of v1, /device:TPU:0, one launch (start us, length us, event | category | flops | bytes accessed | tf_op | source)
XLA Modules:
  0.0 217.4 jit_solution(14637820728655598038)
XLA Ops:
  7.2 0.0 copy-start
  7.2 0.0 copy-start.4
  7.2 0.0 all-reduce.6.cloned.1.call-start
  7.2 0.9 copy-done
  8.1 1.1 multiply_convert_fusion
  9.2 0.0 copy-done.4
  9.3 0.8 fusion.58
  10.0 0.0 all-reduce.6.cloned.1.call-update
  10.1 0.0 all-reduce.8.cloned.1.call-start
  10.1 0.0 copy-start.5
  10.1 0.6 copy-done.5
  10.8 0.6 fusion.51
  12.1 0.0 copy-start.6
  12.1 0.6 copy-done.6
  12.8 0.1 dynamic_slice.31
  12.8 0.1 dynamic_slice.32
  12.9 0.1 select_reduce_fusion
  13.0 0.0 copy-start.7
  13.0 0.6 copy-done.7
  13.7 0.6 dynamic-slice.3
  14.9 19.6 %all-reduce.6.cloned.1.call-done = f32[128,128]{1,0:T(8,128)} async-done(((f32[128,128]{1,0:T(8,128)}), f32[128,128]{1,0:T(8,128)}) %all-reduce.6.cloned.1.call-update) | async-done | bytes 65552 | tf_op jit(solution)/shard_map/psum | solution.py:30
  34.5 0.0 copy-start.1
  34.5 1.0 multiply_reduce_fusion.1
  35.6 0.0 copy-done.1
  35.6 0.1 fusion.57
  35.7 21.7 %all_gather.19 = bf16[512,128]{1,0:T(8,128)(2,1)S(1)} all-gather(bf16[32,128]{1,0:T(8,128)(2,1)S(1)} %constant_dynamic-slice_fusion.1), channel_id=1, replica_groups=mesh['dp'=16,'mp'=2] {'dp'}, dimensions={0}, use_global_device_ids=true | all-gather | bytes 139264 | tf_op jit(solution)/shard_map/all_gather | solution.py:86
  57.4 18.1 %all_gather.17 = bf16[1024,128]{1,0:T(8,128)(2,1)S(1)} all-gather(bf16[64,128]{1,0:T(8,128)(2,1)S(1)} %constant_dynamic-slice_fusion), channel_id=1, replica_groups=mesh['dp'=16,'mp'=2] {'dp'}, dimensions={0}, use_global_device_ids=true | all-gather | bytes 278528 | tf_op jit(solution)/shard_map/all_gather | solution.py:35
  75.5 0.3 fusion.12
  75.8 4.9 %all-reduce.2 = (f32[32]{0:T(128)S(1)}, f32[32]{0:T(128)S(1)}) all-reduce(f32[32]{0:T(128)S(1)} %get-tuple-element.83, f32[32]{0:T(128)S(1)} %get-tuple-element.82), channel_id=1, replica_groups=mesh['dp'=16,'mp'=2] {'mp'}, use_global_device_ids=true, to_apply=%region_6.7 | all-reduce | flops 64 | bytes 512 | tf_op jit(solution)/shard_map/psum | solution.py:64
  80.8 0.2 dynamic-update-slice.2
  81.0 29.9 %all-reduce = f32[512]{0:T(512)S(1)} all-reduce(f32[512]{0:T(512)S(1)} %dynamic-update-slice.2), channel_id=1, replica_groups=mesh['dp'=16,'mp'=2] {'dp'}, use_global_device_ids=true, to_apply=%add | all-reduce | flops 512 | bytes 4096
  110.9 0.2 convolution_dynamic-update-slice_fusion
  111.1 0.3 fusion.11
  111.5 4.9 %all_gather.22 = f32[2,128,128]{2,1,0:T(8,128)S(1)} all-gather(f32[1,128,128]{2,1,0:T(8,128)S(1)} %fusion.11), channel_id=1, replica_groups=mesh['dp'=16,'mp'=2] {'mp'}, dimensions={0}, use_global_device_ids=true | all-gather | bytes 196608 | tf_op jit(solution)/shard_map/all_gather | solution.py:116
  116.4 0.2 multiply_reduce_fusion
  116.6 0.1 divide_convert_fusion
  116.7 0.9 fusion.59
  117.6 0.0 copy-start.3
  117.6 0.2 convert_reduce_fusion
  117.8 0.7 copy-done.3
  118.5 1.0 convolution_bitcast_fusion
  119.5 0.0 all-reduce.8.cloned.1.call-update
  119.5 30.2 %psum.46 = f32[256]{0:T(256)} all-reduce(f32[256]{0:T(256)S(1)} %get-tuple-element.100), channel_id=1, replica_groups=mesh['dp'=16,'mp'=2] {'dp'}, use_global_device_ids=true, to_apply=%region_12.13 | all-reduce | flops 256 | bytes 2048 | tf_op jit(solution)/shard_map/psum | solution.py:129
  149.7 0.5 add_subtract_fusion
  150.3 57.6 %all-reduce.8.cloned.1.call-done = (f32[512,256]{0,1:T(8,128)}, f32[256,128]{1,0:T(8,128)}) async-done(((f32[512,256]{0,1:T(8,128)}, f32[256,128]{1,0:T(8,128)}), (f32[512,256]{0,1:T(8,128)}, f32[256,128]{1,0:T(8,128)})) %all-reduce.8.cloned.1.call-update) | async-done | bytes 655376 | tf_op jit(solution)/shard_map/psum | solution.py:129
  207.9 0.0 copy-start.2
  207.9 2.1 copy.12
  209.9 0.0 copy-done.2
  209.9 0.7 copy.19
  (12 shorter events, 0.1 us)
Async XLA Ops:
  7.2 1.0 copy-start
  7.2 2.1 copy-start.4
  7.2 27.3 %all-reduce.6.cloned.1.call-start = ((), (), s32[]{:S(2)}) async-start(), calls=%async_computation | async-start | bytes 131072 | tf_op jit(solution)/shard_map/psum | solution.py:30
  10.1 197.8 %all-reduce.8.cloned.1.call-start = ((), (), s32[]{:S(2)}) async-start(), calls=%async_computation.1 | async-start | bytes 1310720 | tf_op jit(solution)/shard_map/psum | solution.py:129
  10.1 0.7 copy-start.5
  12.1 0.7 copy-start.6
  13.0 0.7 copy-start.7
  34.5 1.0 copy-start.1
  117.6 0.9 copy-start.3
  207.9 2.1 copy-start.2
Sparse Core Ops, SparseCore 0:
  10.8 23.6 all-reduce.5
  119.7 88.1 all-reduce.7
